TPU v7x, 32 devices: a whole 2x2x4 slice. The times are simulated.
32 devices in a mesh: layer: 8 (over z, x), land: 4 (over y, core).
Axes of the slice: x: 2, y: 2, z: 4, core: 2. Of those that a mesh axis runs over, the one named last changes fastest.
Arguments:
- gradients: bfloat16 [960, 65536], P(None, ('layer', 'land')), may hold values from -6 to 6
- queries: bfloat16 [32, 65536], P(None, ('layer', 'land')), may hold values from -6 to 6
- landmarks: bfloat16 [1024, 65536], P(None, ('layer', 'land')), may hold values from -0.0234375 to 0.0234375
- whitening: bfloat16 [1024, 1024], P(None, 'land'), may hold values from -2.5 to 2.5
Outputs:
- scores: float32 [32, 960], P('land', 'layer')
All inputs are finite; a program needn't handle non-finite values.
Results may differ from a plain program's by a relative error of at most 0.023.
Values may be sent and summed in bfloat16 or wider, within the bound.
A program may use at most 128 MiB of HBM per device.

v0:
```python
import jax
import jax.numpy as jnp
from jax import lax
from jax.sharding import PartitionSpec as P

LANDMARKS = 1024


def contract_rows(rows, piece):
    return lax.dot_general(
        rows, piece, (((1,), (1,)), ((), ())), preferred_element_type=jnp.float32
    )


def make_folder(example_rows, query_rows, piece):
    return (contract_rows(example_rows, piece), contract_rows(query_rows, piece))


def local(gradients, queries, landmarks, whitening):
    n_layer = lax.axis_size("layer")
    n_land = lax.axis_size("land")
    width = gradients.shape[1]
    rows_each = gradients.shape[0] // (n_layer * n_land)
    query_each = queries.shape[0] // (n_layer * n_land)
    split_ex = gradients.reshape(n_layer, n_land, rows_each, width)
    split_qr = queries.reshape(n_layer, n_land, query_each, width)
    moved_ex, moved_qr = (
        lax.all_to_all(split_ex, "land", split_axis=1, concat_axis=3, tiled=True),
        lax.all_to_all(split_qr, "land", split_axis=1, concat_axis=3, tiled=True),
    )
    layer_rows = moved_ex.reshape(n_layer * rows_each, n_land * width)
    layer_query = moved_qr.reshape(n_layer * query_each, n_land * width)
    partial_ex, partial_qr = make_folder(
        layer_rows, layer_query, lax.all_gather(landmarks, "land", axis=1, tiled=True)
    )
    share_ex, share_qr = (
        lax.psum_scatter(
            partial_ex.astype(jnp.bfloat16), "layer", scatter_dimension=0, tiled=True
        ).astype(jnp.float32),
        lax.psum_scatter(
            partial_qr.astype(jnp.bfloat16), "layer", scatter_dimension=0, tiled=True
        ).astype(jnp.float32),
    )
    projected, query_proj = (
        lax.all_gather(share_ex.astype(jnp.bfloat16), "land", axis=0, tiled=True),
        lax.all_gather(share_qr.astype(jnp.bfloat16), "land", axis=0, tiled=True),
    )
    whitened = jnp.dot(projected, whitening, preferred_element_type=jnp.float32).astype(
        jnp.bfloat16
    )
    query_white = jnp.dot(query_proj, whitening, preferred_element_type=jnp.float32).astype(
        jnp.bfloat16
    )
    all_queries = lax.all_gather(query_white, "layer", axis=0, tiled=True)
    factor = LANDMARKS ** (-0.5)
    return lax.psum_scatter(
        (contract_rows(all_queries, whitened) * factor).astype(jnp.bfloat16),
        "land",
        scatter_dimension=0,
        tiled=True,
    ).astype(jnp.float32)


def solution(mesh):
    return jax.shard_map(
        local,
        mesh=mesh,
        in_specs=(
            P(None, ("layer", "land")),
            P(None, ("layer", "land")),
            P(None, ("layer", "land")),
            P(None, "land"),
        ),
        out_specs=P("land", "layer"),
        check_vma=False,
    )
```

profile of v0, /device:TPU:0, one launch (start us, length us, event | category | flops | bytes accessed | tf_op | source)
XLA Modules:
  0.0 296.0 jit_solution(8832669708729953579)
XLA Ops:
  6.5 0.0 copy-start
  6.5 0.0 all-gather.5.cloned.1.call-start
  6.5 0.7 all-gather.5.cloned.1.call-update
  7.3 5.0 %reshape.19 = bf16[8,4,30,2048]{3,2,1,0:T(8,128)(2,1)} reshape(bf16[960,2048]{1,0:T(8,128)(2,1)} %param.4) | data formatting | bytes 7864320 | tf_op jit(solution)/shard_map/reshape | solution.py:25
  12.3 6.4 %copy.9 = bf16[8,4,30,2048]{3,0,2,1:T(8,128)(2,1)} copy(bf16[8,4,30,2048]{3,2,1,0:T(8,128)(2,1)} %reshape.19) | data formatting | bytes 7864320 | tf_op jit(solution)/shard_map/reshape | solution.py:25
  18.7 0.0 copy-start.1
  18.7 0.0 copy-start.3
  18.7 0.0 copy-start.2
  18.7 5.1 %all-to-all-start.1 = ((bf16[8,4,30,2048]{3,0,2,1:T(8,128)(2,1)}), bf16[8,4,30,2048]{3,0,2,1:T(8,128)(2,1)}, u32[]{:S(2)}, u32[]{:S(2)}) async-start(bf16[8,4,30,2048]{3,0,2,1:T(8,128)(2,1)} %copy.9), calls=%async_computation.1 | async-start | bytes 7864320 | tf_op jit(solution)/shard_map/all_to_all | solution.py:28
  23.8 0.0 copy-done.1
  23.8 0.1 reshape.17
  23.9 0.7 copy.8
  24.6 0.0 copy-done.3
  24.6 0.6 dynamic-slice.4
  25.2 0.0 copy-done.2
  25.2 0.7 fusion.7
  27.1 85.5 %all-to-all-done.1 = bf16[8,4,30,2048]{3,0,2,1:T(8,128)(2,1)} async-done(((bf16[8,4,30,2048]{3,0,2,1:T(8,128)(2,1)}), bf16[8,4,30,2048]{3,0,2,1:T(8,128)(2,1)}, u32[]{:S(2)}, u32[]{:S(2)}) %all-to-all-start.1) | async-done | bytes 3932192 | tf_op jit(solution)/shard_map/all_to_all | solution.py:28
  112.6 3.5 %all-to-all-start = ((bf16[8,4,1,2048]{3,0,2,1:T(8,128)(2,1)}), bf16[8,4,1,2048]{3,0,2,1:T(8,128)(2,1)S(1)}, u32[]{:S(2)}, u32[]{:S(2)}) async-start(bf16[8,4,1,2048]{3,0,2,1:T(8,128)(2,1)} %copy.8), calls=%async_computation | async-start | bytes 262144 | tf_op jit(solution)/shard_map/all_to_all | solution.py:29
  116.1 5.1 %copy.10 = bf16[8,1,30,4,2048]{4,3,2,0,1:T(4,128)(2,1)S(1)} copy(bf16[8,1,30,4,2048]{4,0,2,3,1:T(8,128)(2,1)} %bitcast.4) | data formatting | bytes 7864320 | tf_op jit(solution)/shard_map/all_to_all | solution.py:28
  121.2 6.0 %copy.12 = bf16[30,8,4,2048]{3,1,2,0:T(8,128)(2,1)} copy(bf16[30,8,4,2048]{3,2,1,0:T(4,128)(2,1)S(1)} %bitcast.29) | data formatting | bytes 7864320
  127.2 33.9 %all-gather.5.cloned.1.call-done = bf16[1024,8192]{1,0:T(8,128)(2,1)} async-done(((bf16[1024,2048]{1,0:T(8,128)(2,1)}), bf16[1024,8192]{1,0:T(8,128)(2,1)}) %all-gather.5.cloned.1.call-update) | async-done | bytes 16777232 | tf_op jit(solution)/shard_map/all_gather | solution.py:34
  161.1 11.5 %convolution_convert_fusion = bf16[240,1024]{1,0:T(8,128)(2,1)S(1)} fusion(bf16[240,8192]{1,0:T(8,128)(2,1)} %bitcast.30, bf16[1024,8192]{1,0:T(8,128)(2,1)} %all-gather.5.cloned.1.call-done), kind=kOutput, calls=%fused_computation | convolution fusion | flops 4026777600 | bytes 21200896 | tf_op jit(solution)/shard_map/dot_general | solution.py:10
  172.6 25.3 %fusion = bf16[32,1024]{1,0:T(8,128)(2,1)S(1)} fusion(bf16[240,1024]{1,0:T(8,128)(2,1)S(1)} %convolution_convert_fusion), kind=kCustom, calls=%all-reduce-scatter | all-reduce-scatter fusion | flops 262145 | bytes 557568
  197.9 2.1 collective-permute-start
  200.0 0.0 all-to-all-done
  200.0 10.2 %convolution_convert_fusion.2 = bf16[8,1024]{1,0:T(8,128)(2,1)S(1)} fusion(bf16[8,8192]{1,0:T(8,128)(2,1)S(1)} %bitcast.31, bf16[1024,8192]{1,0:T(8,128)(2,1)} %all-gather.5.cloned.1.call-done), kind=kOutput, calls=%fused_computation.3 | convolution fusion | flops 134225920 | bytes 16924672 | tf_op jit(solution)/shard_map/dot_general | solution.py:10
  210.2 33.6 %all-reduce = bf16[8,1024]{1,0:T(8,128)(2,1)S(1)} all-reduce(bf16[8,1024]{1,0:T(8,128)(2,1)S(1)} %convolution_convert_fusion.2), channel_id=2, replica_groups=mesh['layer'=8,'land'=4] {'layer'}, use_global_device_ids=true, to_apply=%region_0.0.clone | all-reduce | flops 8192 | bytes 32768
  243.8 0.6 dynamic-slice_bitcast_fusion.1
  244.4 5.2 %all-gather = bf16[4,1,1024]{2,1,0:T(2,128)(2,1)S(1)} all-gather(bf16[1,1,1024]{2,1,0:T(2,128)(2,1)S(1)} %dynamic-slice_bitcast_fusion.1), channel_id=1, replica_groups=mesh['layer'=8,'land'=4] {'land'}, dimensions={0}, use_global_device_ids=true | all-gather | bytes 10240 | tf_op jit(solution)/shard_map/all_gather | solution.py:46
  249.6 0.0 copy-done
  249.6 0.2 fusion.4
  249.8 26.0 %all-gather.1 = bf16[8,4,256]{2,1,0:T(4,128)(2,1)S(1)} all-gather(bf16[1,4,256]{2,1,0:T(4,128)(2,1)S(1)} %fusion.4), channel_id=1, replica_groups=mesh['layer'=8,'land'=4] {'layer'}, dimensions={0}, use_global_device_ids=true | all-gather | bytes 18432 | tf_op jit(solution)/shard_map/all_gather | solution.py:54
  275.8 0.0 collective-permute-done
  275.8 0.2 concatenate
  276.1 5.8 %all-gather.2 = bf16[4,30,1024]{2,1,0:T(8,128)(2,1)S(1)} all-gather(bf16[1,30,1024]{2,1,0:T(8,128)(2,1)S(1)} %dynamic-slice_bitcast_fusion), channel_id=1, replica_groups=mesh['layer'=8,'land'=4] {'land'}, dimensions={0}, use_global_device_ids=true | all-gather | bytes 307200 | tf_op jit(solution)/shard_map/all_gather | solution.py:45
  281.9 0.1 reshape.26
  281.9 0.3 fusion.3
  282.3 6.2 %all-reduce.2 = bf16[32,120]{1,0:T(8,128)(2,1)S(1)} all-reduce(bf16[32,120]{1,0:T(8,128)(2,1)S(1)} %fusion.3), channel_id=4, replica_groups=mesh['layer'=8,'land'=4] {'land'}, use_global_device_ids=true, to_apply=%region_2.0.clone | all-reduce | flops 3840 | bytes 15360
  288.5 0.6 dynamic-slice_convert_fusion
  (3 shorter events, 0.1 us)
Async XLA Ops:
  6.5 243.1 %copy-start = (bf16[1024,256]{1,0:T(8,128)(2,1)S(1)}, bf16[1024,256]{1,0:T(8,128)(2,1)}, u32[]{:S(2)}) copy-start(bf16[1024,256]{1,0:T(8,128)(2,1)} %param.7) | copy-start | bytes 1572868
  6.5 154.6 %all-gather.5.cloned.1.call-start = ((), (), s32[]{:S(2)}) async-start(), calls=%async_computation.2 | async-start | bytes 20971520 | tf_op jit(solution)/shard_map/all_gather | solution.py:34
  18.7 5.1 %copy-start.1 = (bf16[32,2048]{1,0:T(8,128)(2,1)S(1)}, bf16[32,2048]{1,0:T(8,128)(2,1)}, u32[]{:S(2)}) copy-start(bf16[32,2048]{1,0:T(8,128)(2,1)} %param.5) | copy-start | bytes 393220
  18.7 6.0 %copy-start.3 = (u32[32]{0:T(128)S(1)}, u32[32]{0:T(128)}, u32[]{:S(2)}) copy-start(u32[32]{0:T(128)} %constant.12) | copy-start | bytes 388
  18.7 6.5 %copy-start.2 = (u32[32]{0:T(128)S(1)}, u32[32]{0:T(128)}, u32[]{:S(2)}) copy-start(u32[32]{0:T(128)} %constant.4) | copy-start | bytes 388
  18.7 93.9 %all-to-all-start.1 = ((bf16[8,4,30,2048]{3,0,2,1:T(8,128)(2,1)}), bf16[8,4,30,2048]{3,0,2,1:T(8,128)(2,1)}, u32[]{:S(2)}, u32[]{:S(2)}) async-start(bf16[8,4,30,2048]{3,0,2,1:T(8,128)(2,1)} %copy.9), calls=%async_computation.1 | async-start | bytes 7864320 | tf_op jit(solution)/shard_map/all_to_all | solution.py:28
  112.6 87.4 %all-to-all-start = ((bf16[8,4,1,2048]{3,0,2,1:T(8,128)(2,1)}), bf16[8,4,1,2048]{3,0,2,1:T(8,128)(2,1)S(1)}, u32[]{:S(2)}, u32[]{:S(2)}) async-start(bf16[8,4,1,2048]{3,0,2,1:T(8,128)(2,1)} %copy.8), calls=%async_computation | async-start | bytes 262144 | tf_op jit(solution)/shard_map/all_to_all | solution.py:29
  197.9 77.9 %collective-permute-start = (bf16[14,1024]{1,0:T(8,128)(2,1)S(1)}, bf16[14,1024]{1,0:T(8,128)(2,1)S(1)}, u32[]{:S(2)}, u32[]{:S(2)}) collective-permute-start(bf16[14,1024]{1,0:T(8,128)(2,1)S(1)} %slice), channel_id=1, source_target_pairs={{0,4},{4,8},{8,12},{12,16},{16,20},{20,24},{24,28},{1,5},{5,9},{9,... | collective-permute-start | bytes 86024
Sparse Core Ops, SparseCore 0:
  8.9 152.1 all-gather.4
where the time goes:
time: 297 us; the launch traced here: 296 us
  waiting for transfers between devices  120 us (40%)
  blocking collectives  102 us (34%)
  local copies, waits for them, and re-layouts  25.6 us (9%)
  matrix products  22.2 us (7%)
  between operations  14.8 us (5%)
  starting transfers between devices  10.7 us (4%)
    all_to_all x1, waiting for transfers between devices, local(): lax.all_to_all(split_ex, 'land', split_axis=1, concat_axis=3, tiled=True)  85.5 us
    unnamed x3, blocking collectives  65.1 us
    all_gather x1, waiting for transfers between devices, local(): lax.all_gather(landmarks, 'land', axis=1, tiled=True)  33.9 us
    all_gather x1, blocking collectives, local(): all_queries = lax.all_gather(query_white, 'layer', axis=0, tiled=True)  26 us
    dot_general x3, matrix products, contract_rows(): lax.dot_general(rows, piece, (((1,), (1,)), ((), ())), preferred_element_...  22 us
    reshape x2, local copies, waits for them, and re-layouts, local(): split_ex = gradients.reshape(n_layer, n_land, rows_each, width)  11.4 us
    unnamed x17, local copies, waits for them, and re-layouts  8.18 us
  transfers between devices with their start and end apart: 4, of which 2 were waited for; matrix products, arithmetic and copies ran while one was open for 24% of the time, Pallas kernels for 0%

commit v1 on v0

--- a/solution.py
+++ b/solution.py
@@ -51,7 +51,14 @@
     query_white = jnp.dot(query_proj, whitening, preferred_element_type=jnp.float32).astype(
         jnp.bfloat16
     )
-    all_queries = lax.all_gather(query_white, "layer", axis=0, tiled=True)
+    ring = [query_white]
+    for hop in range(7):
+        ring.append(lax.ppermute(ring[-1], "layer", [(dev, (dev + 1) % 8) for dev in range(8)]))
+    all_queries = jnp.roll(
+        jnp.concatenate(ring[::-1], axis=0),
+        (lax.axis_index("layer") + 1) * ring[0].shape[0],
+        axis=0,
+    )
     factor = LANDMARKS ** (-0.5)
     return lax.psum_scatter(
         (contract_rows(all_queries, whitened) * factor).astype(jnp.bfloat16),

time: 297 us -> 315 us (1.061)
  waiting for transfers between devices: 120 us -> 164 us
  blocking collectives: 102 us -> 76.1 us
    ppermute x0 -> x7, waiting for transfers between devices: none -> 42 us  [local(): lax.ppermute(ring[-1], 'layer', [(dev, (dev + 1) % 8) for dev in range(8)])]
    all_gather x1 -> x0, blocking collectives: 26 us -> none  [local(): all_queries = lax.all_gather(query_white, 'layer', axis=0, tiled=True)]
    unnamed x17 -> x16, local copies, waits for them, and re-layouts: 8.18 us -> 8.2 us
  transfers between devices with their start and end apart: 4 -> 11, of which waited for: 2 -> 9; matrix products, arithmetic and copies ran while one was open for 24% -> 23% of each run, Pallas kernels for 0% -> 0%
where the time goes in v1:
time: 315 us; the launch traced here: 314 us
  waiting for transfers between devices  164 us (52%)
  blocking collectives  76.1 us (24%)
  local copies, waits for them, and re-layouts  25.8 us (8%)
  matrix products  22.2 us (7%)
  between operations  14.9 us (5%)
  starting transfers between devices  10.7 us (3%)
    all_to_all x1, waiting for transfers between devices, local(): lax.all_to_all(split_ex, 'land', split_axis=1, concat_axis=3, tiled=True)  87.3 us
    unnamed x3, blocking collectives  65.1 us
    ppermute x7, waiting for transfers between devices, local(): lax.ppermute(ring[-1], 'layer', [(dev, (dev + 1) % 8) for dev in range(8)])  42 us
    all_gather x1, waiting for transfers between devices, local(): lax.all_gather(landmarks, 'land', axis=1, tiled=True)  33.9 us
    dot_general x3, matrix products, contract_rows(): lax.dot_general(rows, piece, (((1,), (1,)), ((), ())), preferred_element_...  22 us
    reshape x2, local copies, waits for them, and re-layouts, local(): split_ex = gradients.reshape(n_layer, n_land, rows_each, width)  11.4 us
    unnamed x16, local copies, waits for them, and re-layouts  8.2 us
  transfers between devices with their start and end apart: 11, of which 9 were waited for; matrix products, arithmetic and copies ran while one was open for 23% of the time, Pallas kernels for 0%

profile of v1, /device:TPU:0, one launch (start us, length us, event | category | flops | bytes accessed | tf_op | source)
XLA Modules:
  0.0 314.2 jit_solution(12606751874489329123)
XLA Ops:
  6.5 0.0 copy-start
  6.5 0.0 all-gather.4.cloned.1.call-start
  6.5 0.7 all-gather.4.cloned.1.call-update
  7.3 5.1 %reshape.19 = bf16[8,4,30,2048]{3,2,1,0:T(8,128)(2,1)} reshape(bf16[960,2048]{1,0:T(8,128)(2,1)} %param.4) | data formatting | bytes 7864320 | tf_op jit(solution)/shard_map/reshape | solution.py:25
  12.3 6.4 %copy.9 = bf16[8,4,30,2048]{3,0,2,1:T(8,128)(2,1)} copy(bf16[8,4,30,2048]{3,2,1,0:T(8,128)(2,1)} %reshape.19) | data formatting | bytes 7864320 | tf_op jit(solution)/shard_map/reshape | solution.py:25
  18.7 5.1 %all-to-all-start.1 = ((bf16[8,4,30,2048]{3,0,2,1:T(8,128)(2,1)}), bf16[8,4,30,2048]{3,0,2,1:T(8,128)(2,1)}, u32[]{:S(2)}, u32[]{:S(2)}) async-start(bf16[8,4,30,2048]{3,0,2,1:T(8,128)(2,1)} %copy.9), calls=%async_computation.1 | async-start | bytes 7864320 | tf_op jit(solution)/shard_map/all_to_all | solution.py:28
  23.8 0.0 copy-done.1
  23.8 0.1 reshape.17
  23.9 0.7 copy.8
  24.6 0.7 fusion.8
  25.3 87.3 %all-to-all-done.1 = bf16[8,4,30,2048]{3,0,2,1:T(8,128)(2,1)} async-done(((bf16[8,4,30,2048]{3,0,2,1:T(8,128)(2,1)}), bf16[8,4,30,2048]{3,0,2,1:T(8,128)(2,1)}, u32[]{:S(2)}, u32[]{:S(2)}) %all-to-all-start.1) | async-done | bytes 3932192 | tf_op jit(solution)/shard_map/all_to_all | solution.py:28
  112.6 3.5 %all-to-all-start = ((bf16[8,4,1,2048]{3,0,2,1:T(8,128)(2,1)}), bf16[8,4,1,2048]{3,0,2,1:T(8,128)(2,1)S(1)}, u32[]{:S(2)}, u32[]{:S(2)}) async-start(bf16[8,4,1,2048]{3,0,2,1:T(8,128)(2,1)} %copy.8), calls=%async_computation | async-start | bytes 262144 | tf_op jit(solution)/shard_map/all_to_all | solution.py:29
  116.1 5.1 %copy.10 = bf16[8,1,30,4,2048]{4,3,2,0,1:T(4,128)(2,1)S(1)} copy(bf16[8,1,30,4,2048]{4,0,2,3,1:T(8,128)(2,1)} %bitcast.3) | data formatting | bytes 7864320 | tf_op jit(solution)/shard_map/all_to_all | solution.py:28
  121.3 6.0 %copy.12 = bf16[30,8,4,2048]{3,1,2,0:T(8,128)(2,1)} copy(bf16[30,8,4,2048]{3,2,1,0:T(4,128)(2,1)S(1)} %bitcast.26) | data formatting | bytes 7864320
  127.2 33.9 %all-gather.4.cloned.1.call-done = bf16[1024,8192]{1,0:T(8,128)(2,1)} async-done(((bf16[1024,2048]{1,0:T(8,128)(2,1)}), bf16[1024,8192]{1,0:T(8,128)(2,1)}) %all-gather.4.cloned.1.call-update) | async-done | bytes 16777232 | tf_op jit(solution)/shard_map/all_gather | solution.py:34
  161.1 11.5 %convolution_convert_fusion = bf16[240,1024]{1,0:T(8,128)(2,1)S(1)} fusion(bf16[240,8192]{1,0:T(8,128)(2,1)} %bitcast.27, bf16[1024,8192]{1,0:T(8,128)(2,1)} %all-gather.4.cloned.1.call-done), kind=kOutput, calls=%fused_computation | convolution fusion | flops 4026777600 | bytes 21200896 | tf_op jit(solution)/shard_map/dot_general | solution.py:10
  172.6 25.3 %fusion = bf16[32,1024]{1,0:T(8,128)(2,1)S(1)} fusion(bf16[240,1024]{1,0:T(8,128)(2,1)S(1)} %convolution_convert_fusion), kind=kCustom, calls=%all-reduce-scatter | all-reduce-scatter fusion | flops 262145 | bytes 557568
  197.9 2.1 collective-permute-start.7
  200.0 0.0 all-to-all-done
  200.0 0.0 copy-start.3
  200.0 10.2 %convolution_convert_fusion.2 = bf16[8,1024]{1,0:T(8,128)(2,1)S(1)} fusion(bf16[8,8192]{1,0:T(8,128)(2,1)S(1)} %bitcast.28, bf16[1024,8192]{1,0:T(8,128)(2,1)} %all-gather.4.cloned.1.call-done), kind=kOutput, calls=%fused_computation.3 | convolution fusion | flops 134225920 | bytes 16924672 | tf_op jit(solution)/shard_map/dot_general | solution.py:10
  210.2 33.6 %all-reduce = bf16[8,1024]{1,0:T(8,128)(2,1)S(1)} all-reduce(bf16[8,1024]{1,0:T(8,128)(2,1)S(1)} %convolution_convert_fusion.2), channel_id=2, replica_groups=mesh['layer'=8,'land'=4] {'layer'}, use_global_device_ids=true, to_apply=%region_0.0.clone | all-reduce | flops 8192 | bytes 32768
  243.8 0.7 dynamic-slice_bitcast_fusion.1
  244.5 5.2 %all-gather = bf16[4,1,1024]{2,1,0:T(2,128)(2,1)S(1)} all-gather(bf16[1,1,1024]{2,1,0:T(2,128)(2,1)S(1)} %dynamic-slice_bitcast_fusion.1), channel_id=1, replica_groups=mesh['layer'=8,'land'=4] {'land'}, dimensions={0}, use_global_device_ids=true | all-gather | bytes 10240 | tf_op jit(solution)/shard_map/all_gather | solution.py:46
  249.7 0.2 convolution_convert_fusion.3
  249.8 0.0 collective-permute-start
  249.8 6.3 %collective-permute-done = bf16[4,256]{1,0:T(4,128)(2,1)S(1)} collective-permute-done((bf16[4,256]{1,0:T(4,128)(2,1)S(1)}, bf16[4,256]{1,0:T(4,128)(2,1)S(1)}, u32[]{:S(2)}, u32[]{:S(2)}) %collective-permute-start) | collective-permute-done | bytes 2080 | tf_op jit(solution)/shard_map/ppermute | solution.py:56
  256.1 0.0 collective-permute-start.1
  256.1 6.3 %collective-permute-done.1 = bf16[4,256]{1,0:T(4,128)(2,1)S(1)} collective-permute-done((bf16[4,256]{1,0:T(4,128)(2,1)S(1)}, bf16[4,256]{1,0:T(4,128)(2,1)S(1)}, u32[]{:S(2)}, u32[]{:S(2)}) %collective-permute-start.1) | collective-permute-done | bytes 2080 | tf_op jit(solution)/shard_map/ppermute | solution.py:56
  262.4 0.0 collective-permute-start.2
  262.4 6.3 %collective-permute-done.2 = bf16[4,256]{1,0:T(4,128)(2,1)S(1)} collective-permute-done((bf16[4,256]{1,0:T(4,128)(2,1)S(1)}, bf16[4,256]{1,0:T(4,128)(2,1)S(1)}, u32[]{:S(2)}, u32[]{:S(2)}) %collective-permute-start.2) | collective-permute-done | bytes 2080 | tf_op jit(solution)/shard_map/ppermute | solution.py:56
  268.7 0.0 collective-permute-start.3
  268.7 6.3 %collective-permute-done.3 = bf16[4,256]{1,0:T(4,128)(2,1)S(1)} collective-permute-done((bf16[4,256]{1,0:T(4,128)(2,1)S(1)}, bf16[4,256]{1,0:T(4,128)(2,1)S(1)}, u32[]{:S(2)}, u32[]{:S(2)}) %collective-permute-start.3) | collective-permute-done | bytes 2080 | tf_op jit(solution)/shard_map/ppermute | solution.py:56
  275.0 0.0 collective-permute-start.4
  275.0 6.3 %collective-permute-done.4 = bf16[4,256]{1,0:T(4,128)(2,1)S(1)} collective-permute-done((bf16[4,256]{1,0:T(4,128)(2,1)S(1)}, bf16[4,256]{1,0:T(4,128)(2,1)S(1)}, u32[]{:S(2)}, u32[]{:S(2)}) %collective-permute-start.4) | collective-permute-done | bytes 2080 | tf_op jit(solution)/shard_map/ppermute | solution.py:56
  281.3 0.0 collective-permute-start.5
  281.3 6.3 %collective-permute-done.5 = bf16[4,256]{1,0:T(4,128)(2,1)S(1)} collective-permute-done((bf16[4,256]{1,0:T(4,128)(2,1)S(1)}, bf16[4,256]{1,0:T(4,128)(2,1)S(1)}, u32[]{:S(2)}, u32[]{:S(2)}) %collective-permute-start.5) | collective-permute-done | bytes 2080 | tf_op jit(solution)/shard_map/ppermute | solution.py:56
  287.6 0.0 collective-permute-start.6
  287.6 0.6 dynamic-slice.4
  289.5 4.4 %collective-permute-done.6 = bf16[4,256]{1,0:T(4,128)(2,1)S(1)} collective-permute-done((bf16[4,256]{1,0:T(4,128)(2,1)S(1)}, bf16[4,256]{1,0:T(4,128)(2,1)S(1)}, u32[]{:S(2)}, u32[]{:S(2)}) %collective-permute-start.6) | collective-permute-done | bytes 2080 | tf_op jit(solution)/shard_map/ppermute | solution.py:56
  293.8 0.2 concatenate.6
  294.0 0.0 collective-permute-done.7
  294.0 0.2 concatenate.7
  294.3 5.8 %all-gather.1 = bf16[4,30,1024]{2,1,0:T(8,128)(2,1)S(1)} all-gather(bf16[1,30,1024]{2,1,0:T(8,128)(2,1)S(1)} %dynamic-slice_bitcast_fusion), channel_id=1, replica_groups=mesh['layer'=8,'land'=4] {'land'}, dimensions={0}, use_global_device_ids=true | all-gather | bytes 307200 | tf_op jit(solution)/shard_map/all_gather | solution.py:45
  300.1 0.1 reshape.24
  300.1 0.4 fusion.3
  300.5 6.2 %all-reduce.2 = bf16[32,120]{1,0:T(8,128)(2,1)S(1)} all-reduce(bf16[32,120]{1,0:T(8,128)(2,1)S(1)} %fusion.3), channel_id=4, replica_groups=mesh['layer'=8,'land'=4] {'land'}, use_global_device_ids=true, to_apply=%region_2.3.clone | all-reduce | flops 3840 | bytes 15360
  306.7 0.6 dynamic-slice_convert_fusion
  (7 shorter events, 0.0 us)
Async XLA Ops:
  6.5 243.1 %copy-start = (bf16[1024,256]{1,0:T(8,128)(2,1)S(1)}, bf16[1024,256]{1,0:T(8,128)(2,1)}, u32[]{:S(2)}) copy-start(bf16[1024,256]{1,0:T(8,128)(2,1)} %param.7) | copy-start | bytes 1572868
  6.5 154.6 %all-gather.4.cloned.1.call-start = ((), (), s32[]{:S(2)}) async-start(), calls=%async_computation.2 | async-start | bytes 20971520 | tf_op jit(solution)/shard_map/all_gather | solution.py:34
  18.7 5.1 %copy-start.1 = (bf16[32,2048]{1,0:T(8,128)(2,1)S(1)}, bf16[32,2048]{1,0:T(8,128)(2,1)}, u32[]{:S(2)}) copy-start(bf16[32,2048]{1,0:T(8,128)(2,1)} %param.5) | copy-start | bytes 393220
  18.7 5.9 %copy-start.2 = (u32[32]{0:T(128)S(1)}, u32[32]{0:T(128)}, u32[]{:S(2)}) copy-start(u32[32]{0:T(128)} %constant.36) | copy-start | bytes 388
  18.7 93.9 %all-to-all-start.1 = ((bf16[8,4,30,2048]{3,0,2,1:T(8,128)(2,1)}), bf16[8,4,30,2048]{3,0,2,1:T(8,128)(2,1)}, u32[]{:S(2)}, u32[]{:S(2)}) async-start(bf16[8,4,30,2048]{3,0,2,1:T(8,128)(2,1)} %copy.9), calls=%async_computation.1 | async-start | bytes 7864320 | tf_op jit(solution)/shard_map/all_to_all | solution.py:28
  112.6 87.4 %all-to-all-start = ((bf16[8,4,1,2048]{3,0,2,1:T(8,128)(2,1)}), bf16[8,4,1,2048]{3,0,2,1:T(8,128)(2,1)S(1)}, u32[]{:S(2)}, u32[]{:S(2)}) async-start(bf16[8,4,1,2048]{3,0,2,1:T(8,128)(2,1)} %copy.8), calls=%async_computation | async-start | bytes 262144 | tf_op jit(solution)/shard_map/all_to_all | solution.py:29
  197.9 96.1 %collective-permute-start.7 = (bf16[14,1024]{1,0:T(8,128)(2,1)S(1)}, bf16[14,1024]{1,0:T(8,128)(2,1)S(1)}, u32[]{:S(2)}, u32[]{:S(2)}) collective-permute-start(bf16[14,1024]{1,0:T(8,128)(2,1)S(1)} %slice), channel_id=1, source_target_pairs={{0,4},{4,8},{8,12},{12,16},{16,20},{20,24},{24,28},{1,5},{5,9},{9,... | collective-permute-start | bytes 86024
  200.0 87.5 %copy-start.3 = (u32[32]{0:T(128)S(1)}, u32[32]{0:T(128)}, u32[]{:S(2)}) copy-start(u32[32]{0:T(128)} %constant.44) | copy-start | bytes 388
  249.8 6.3 %collective-permute-start = (bf16[4,256]{1,0:T(4,128)(2,1)S(1)}, bf16[4,256]{1,0:T(4,128)(2,1)S(1)}, u32[]{:S(2)}, u32[]{:S(2)}) collective-permute-start(bf16[4,256]{1,0:T(4,128)(2,1)S(1)} %convolution_convert_fusion.3), channel_id=1, source_target_pairs={{0,4},{4,8},{8,12},{12,16},{16,20},{20,24},{24,28},{28,0},{1,5},{5... | collective-permute-start | bytes 6152 | tf_op jit(solution)/shard_map/ppermute | solution.py:56
  256.1 6.3 %collective-permute-start.1 = (bf16[4,256]{1,0:T(4,128)(2,1)S(1)}, bf16[4,256]{1,0:T(4,128)(2,1)S(1)}, u32[]{:S(2)}, u32[]{:S(2)}) collective-permute-start(bf16[4,256]{1,0:T(4,128)(2,1)S(1)} %collective-permute-done), channel_id=1, source_target_pairs={{0,4},{4,8},{8,12},{12,16},{16,20},{20,24},{24,28},{28,0},{1,5},{5... | collective-permute-start | bytes 6152 | tf_op jit(solution)/shard_map/ppermute | solution.py:56
  262.4 6.3 %collective-permute-start.2 = (bf16[4,256]{1,0:T(4,128)(2,1)S(1)}, bf16[4,256]{1,0:T(4,128)(2,1)S(1)}, u32[]{:S(2)}, u32[]{:S(2)}) collective-permute-start(bf16[4,256]{1,0:T(4,128)(2,1)S(1)} %collective-permute-done.1), channel_id=1, source_target_pairs={{0,4},{4,8},{8,12},{12,16},{16,20},{20,24},{24,28},{28,0},{1,5},{5... | collective-permute-start | bytes 6152 | tf_op jit(solution)/shard_map/ppermute | solution.py:56
  268.7 6.3 %collective-permute-start.3 = (bf16[4,256]{1,0:T(4,128)(2,1)S(1)}, bf16[4,256]{1,0:T(4,128)(2,1)S(1)}, u32[]{:S(2)}, u32[]{:S(2)}) collective-permute-start(bf16[4,256]{1,0:T(4,128)(2,1)S(1)} %collective-permute-done.2), channel_id=1, source_target_pairs={{0,4},{4,8},{8,12},{12,16},{16,20},{20,24},{24,28},{28,0},{1,5},{5... | collective-permute-start | bytes 6152 | tf_op jit(solution)/shard_map/ppermute | solution.py:56
  275.0 6.3 %collective-permute-start.4 = (bf16[4,256]{1,0:T(4,128)(2,1)S(1)}, bf16[4,256]{1,0:T(4,128)(2,1)S(1)}, u32[]{:S(2)}, u32[]{:S(2)}) collective-permute-start(bf16[4,256]{1,0:T(4,128)(2,1)S(1)} %collective-permute-done.3), channel_id=1, source_target_pairs={{0,4},{4,8},{8,12},{12,16},{16,20},{20,24},{24,28},{28,0},{1,5},{5... | collective-permute-start | bytes 6152 | tf_op jit(solution)/shard_map/ppermute | solution.py:56
  281.3 6.3 %collective-permute-start.5 = (bf16[4,256]{1,0:T(4,128)(2,1)S(1)}, bf16[4,256]{1,0:T(4,128)(2,1)S(1)}, u32[]{:S(2)}, u32[]{:S(2)}) collective-permute-start(bf16[4,256]{1,0:T(4,128)(2,1)S(1)} %collective-permute-done.4), channel_id=1, source_target_pairs={{0,4},{4,8},{8,12},{12,16},{16,20},{20,24},{24,28},{28,0},{1,5},{5... | collective-permute-start | bytes 6152 | tf_op jit(solution)/shard_map/ppermute | solution.py:56
  287.6 6.3 %collective-permute-start.6 = (bf16[4,256]{1,0:T(4,128)(2,1)S(1)}, bf16[4,256]{1,0:T(4,128)(2,1)S(1)}, u32[]{:S(2)}, u32[]{:S(2)}) collective-permute-start(bf16[4,256]{1,0:T(4,128)(2,1)S(1)} %collective-permute-done.5), channel_id=1, source_target_pairs={{0,4},{4,8},{8,12},{12,16},{16,20},{20,24},{24,28},{28,0},{1,5},{5... | collective-permute-start | bytes 6152 | tf_op jit(solution)/shard_map/ppermute | solution.py:56
Sparse Core Ops, SparseCore 0:
  8.9 152.1 all-gather.3
